TPU v7x, 32 devices: a whole 2x2x4 slice. The times are simulated.
32 devices in a mesh: band: 4 (over z), grid: 8 (over y, x, core).
Axes of the slice: x: 2, y: 2, z: 4, core: 2. Of those that a mesh axis runs over, the one named last changes fastest.
Arguments:
- orbitals: bfloat16 [8, 256, 256, 256], P('band', 'grid'), may hold values from -60 to 60
- potential: float32 [256, 256, 256], P('grid'), may hold values from -2 to 1
Outputs:
- rotated: bfloat16 [8, 256, 256, 256], P('band', 'grid')
- projected: float32 [8, 8], replicated
All inputs are finite; a program needn't handle non-finite values. Where the computation divides by a largest or mean magnitude, that divisor is 1e-20 or more.
Results may differ from a plain program's by a relative error of at most 0.0005.
The roundings to bfloat16 on the way count: a program that leaves them out, or rounds other values in their place, can miss the bound.
Values may be sent and summed in bfloat16 or wider, within the bound.
A program may use at most 192 MiB of HBM per device.

v0:
```python
import math

import jax
import jax.numpy as jnp
from jax import lax
from jax.sharding import PartitionSpec as P

NS_ITERS = 6


CENTER = 9.5
HALF_WIDTH = 6.5


def second_derivative(length):
    index = jnp.arange(length, dtype=jnp.int32)
    product = index[:, None] * index[None, :] % length
    angles = product.astype(jnp.float32) * (2.0 * math.pi / length)
    freq = jnp.minimum(index, length - index).astype(jnp.float32)
    weight = -((2.0 * math.pi / length * freq) ** 2) / length
    cosines = jnp.cos(angles)
    sines = jnp.sin(angles)
    matrix = jnp.dot(cosines * weight[None, :], cosines.T, precision=lax.Precision.HIGHEST)
    matrix = matrix + jnp.dot(sines * weight[None, :], sines.T, precision=lax.Precision.HIGHEST)
    return matrix.astype(jnp.bfloat16)


def apply_ham(field, potential, k_x, k_y, k_z):
    depth = field.shape[3]
    term_z = jnp.dot(field.reshape(-1, depth), k_z, preferred_element_type=jnp.float32).reshape(
        field.shape
    )
    term_y = jnp.einsum("oxjz,jy->oxyz", field, k_y, preferred_element_type=jnp.float32)
    derived = jnp.einsum(
        "ojyz,jx->oxyz",
        lax.all_to_all(field, "grid", split_axis=2, concat_axis=1, tiled=True),
        k_x,
        preferred_element_type=jnp.float32,
    ).astype(jnp.bfloat16)
    term_x = lax.all_to_all(derived, "grid", split_axis=1, concat_axis=2, tiled=True)
    return -0.5 * (term_x.astype(jnp.float32) + term_y + term_z) + potential[None] * field.astype(
        jnp.float32
    )


def ritz(correlation, hamil):
    scale = jnp.max(jnp.sum(jnp.abs(correlation), axis=1))
    current = correlation / scale
    identity = jnp.eye(correlation.shape[0], dtype=jnp.float32)
    inverse_root = identity
    for turn_index in range(NS_ITERS):
        turn = 1.5 * identity - 0.5 * jnp.dot(
            inverse_root, current, precision=lax.Precision.HIGHEST
        )
        current = jnp.dot(current, turn, precision=lax.Precision.HIGHEST)
        inverse_root = jnp.dot(turn, inverse_root, precision=lax.Precision.HIGHEST)
    projected = (
        jnp.dot(
            jnp.dot(inverse_root.T, hamil, precision=lax.Precision.HIGHEST),
            inverse_root,
            precision=lax.Precision.HIGHEST,
        )
        / scale
    )
    return (inverse_root.astype(jnp.bfloat16), projected)


def inner_rows(left, right):
    return lax.dot_general(
        left, right, (((1,), (1,)), ((), ())), preferred_element_type=jnp.float32
    )


def per_device(orbitals, potential):
    own = orbitals.shape[0]
    k_x = second_derivative(orbitals.shape[1] * lax.axis_size("grid"))
    k_y = second_derivative(orbitals.shape[2])
    k_z = second_derivative(orbitals.shape[3])
    start_f = orbitals.astype(jnp.float32)
    first = (
        (apply_ham(orbitals, potential, k_x, k_y, k_z) - CENTER * start_f) / HALF_WIDTH
    ).astype(jnp.bfloat16)
    first_f = first.astype(jnp.float32)
    filtered = (
        2.0 * (apply_ham(first, potential, k_x, k_y, k_z) - CENTER * first_f) / HALF_WIDTH - start_f
    ).astype(jnp.bfloat16)
    applied = apply_ham(filtered, potential, k_x, k_y, k_z).astype(jnp.bfloat16)
    gathered = lax.all_gather(filtered, "band", axis=0, tiled=True)
    total = gathered.shape[0]
    flat = gathered.reshape(total, -1)
    s_rows = inner_rows(filtered.reshape(own, -1), flat)
    h_rows = inner_rows(applied.reshape(own, -1), flat)
    s_rows, h_rows = lax.psum((s_rows, h_rows), "grid")
    correlation, hamil = (
        lax.all_gather(s_rows, "band", axis=0, tiled=True),
        lax.all_gather(h_rows, "band", axis=0, tiled=True),
    )
    coeff, projected = ritz(correlation, hamil)
    columns = lax.dynamic_slice_in_dim(coeff, lax.axis_index("band") * own, own, 1)
    mine = lax.dot_general(
        columns, flat, (((0,), (0,)), ((), ())), preferred_element_type=jnp.float32
    )
    rotated = mine.astype(jnp.bfloat16).reshape(filtered.shape)
    return (rotated, projected)


def solution(mesh):
    in_specs = (P("band", "grid", None, None), P("grid", None, None))
    out_specs = (P("band", "grid", None, None), P())
    return jax.shard_map(
        per_device, mesh=mesh, in_specs=in_specs, out_specs=out_specs, check_vma=False
    )
```

profile of v0, /device:TPU:0, one launch (start us, length us, event | category | flops | bytes accessed | tf_op | source)
XLA Modules:
  0.0 1303.1 jit_solution(14852924869631262509)
XLA Ops:
  7.2 11.6 copy.65
  18.7 5.4 all-to-all-start
  24.2 1.4 fusion.40
  25.5 1.4 fusion.22
  26.9 91.7 %all-to-all-done = bf16[2,32,256,256]{3,1,0,2:T(8,128)(2,1)} async-done(((bf16[2,32,256,256]{3,1,0,2:T(8,128)(2,1)}), bf16[2,32,256,256]{3,1,0,2:T(8,128)(2,1)}, u32[]{:S(2)}, u32[]{:S(2)}) %all-to-all-start) | async-done | bytes 8388640 | tf_op jit(solution)/shard_map/all_to_all | solution.py:36
  118.6 8.2 copy.66
  126.8 9.0 convert_bitcast_fusion.2
  135.8 11.5 copy.68
  147.4 5.2 all-to-all-start.1
  152.5 11.5 convolution_bitcast_fusion
  164.0 17.5 %copy.71 = f32[16384,256]{1,0:T(8,128)} copy(f32[16384,256]{0,1:T(8,128)} %convolution_bitcast_fusion) | data formatting | bytes 33554432 | tf_op jit(solution)/shard_map/dot_general | solution.py:30
  181.5 65.1 %all-to-all-done.1 = bf16[2,256,32,256]{3,2,0,1:T(8,128)(2,1)} async-done(((bf16[2,256,32,256]{3,2,0,1:T(8,128)(2,1)}), bf16[2,256,32,256]{3,2,0,1:T(8,128)(2,1)}, u32[]{:S(2)}, u32[]{:S(2)}) %all-to-all-start.1) | async-done | bytes 8388640 | tf_op jit(solution)/shard_map/all_to_all | solution.py:40
  246.6 11.3 copy.69
  257.9 23.2 %fusion.10 = bf16[2,32,256,256]{3,2,1,0:T(8,128)(2,1)} fusion(bf16[2,32,256,256]{3,2,1,0:T(8,128)(2,1)} %param.2, f32[2,32,256,256]{3,2,1,0:T(8,128)} %bitcast.160, f32[2,8,32,32,256]{4,3,1,2,0:T(8,128)} %copy.69, f32[32,256,256]{2,1,0:T(8,128)} %param.3, bf16[256,256]{1,0:T(8,128)(2,1)S(1)} %fusion.22), kind=kOutput, calls=%fused_computation.17 | convolution fusion | flops 2189426688 | bytes 58851328 | tf_op jit(solution)/shard_map/oxjz,jy->oxyz/dot_general | solution.py:33
  281.1 11.4 copy.72
  292.5 100.1 %all_to_all.81 = bf16[2,32,256,256]{3,1,0,2:T(8,128)(2,1)} all-to-all(bf16[2,32,256,256]{3,1,0,2:T(8,128)(2,1)} %copy.72), channel_id=1, replica_groups=mesh['band'=4,'grid'=8] {'grid'}, dimensions={2} | all-to-all | bytes 16777216 | tf_op jit(solution)/shard_map/all_to_all | solution.py:36
  392.6 8.0 copy.73
  400.6 9.0 convert_bitcast_fusion.1
  409.6 11.4 copy.75
  421.0 4.9 all-to-all-start.3
  425.9 0.2 all-gather.4.cloned.1.call-start
  426.2 11.5 fusion.55
  437.6 82.3 %all-to-all-done.3 = bf16[2,256,32,256]{3,2,0,1:T(8,128)(2,1)} async-done(((bf16[2,256,32,256]{3,2,0,1:T(8,128)(2,1)}), bf16[2,256,32,256]{3,2,0,1:T(8,128)(2,1)}, u32[]{:S(2)}, u32[]{:S(2)}) %all-to-all-start.3) | async-done | bytes 8388640 | tf_op jit(solution)/shard_map/all_to_all | solution.py:40
  520.0 11.3 copy.76
  531.3 26.1 %fusion.11 = bf16[2,32,256,256]{3,2,1,0:T(8,128)(2,1)} fusion(bf16[2,32,256,256]{3,2,1,0:T(8,128)(2,1)} %param.2, bf16[2,32,256,256]{3,2,1,0:T(8,128)(2,1)} %fusion.10, f32[2,8,32,32,256]{4,3,1,2,0:T(8,128)} %copy.76, f32[256,2,32,256]{3,0,2,1:T(8,128)} %fusion.55, f32[32,256,256]{2,1,0:T(8,128)} %param.3, bf16[256,256]{1,0:T(8,128)(2,1)S(1)} %fusion.22), kind=kOutput, calls=%fused_computation.18 | convolution fusion | flops 2197815296 | bytes 67239936 | tf_op jit(solution)/shard_map/dot_general | solution.py:30
  557.4 13.7 %copy.81 = bf16[2,32,256,256]{3,1,0,2:T(8,128)(2,1)} copy(bf16[2,32,256,256]{3,2,1,0:T(8,128)(2,1)} %fusion.11) | data formatting | bytes 16777216 | tf_op jit(solution)/shard_map/convert_element_type | solution.py:86
  571.1 100.2 %all_to_all.82 = bf16[2,32,256,256]{3,1,0,2:T(8,128)(2,1)} all-to-all(bf16[2,32,256,256]{3,1,0,2:T(8,128)(2,1)} %copy.81), channel_id=1, replica_groups=mesh['band'=4,'grid'=8] {'grid'}, dimensions={2} | all-to-all | bytes 16777216 | tf_op jit(solution)/shard_map/all_to_all | solution.py:36
  671.3 8.3 copy.82
  679.6 9.0 convert_bitcast_fusion
  688.6 11.6 copy.84
  700.2 5.0 all-to-all-start.5
  705.2 11.5 fusion.50
  716.6 82.6 %all-to-all-done.5 = bf16[2,256,32,256]{3,2,0,1:T(8,128)(2,1)} async-done(((bf16[2,256,32,256]{3,2,0,1:T(8,128)(2,1)}), bf16[2,256,32,256]{3,2,0,1:T(8,128)(2,1)}, u32[]{:S(2)}, u32[]{:S(2)}) %all-to-all-start.5) | async-done | bytes 8388640 | tf_op jit(solution)/shard_map/all_to_all | solution.py:40
  799.2 11.3 copy.85
  810.5 23.3 %fusion.15 = bf16[2,32,256,256]{3,2,1,0:T(8,128)(2,1)} fusion(f32[2,8,32,32,256]{4,3,1,2,0:T(8,128)} %copy.85, f32[256,2,32,256]{3,0,2,1:T(8,128)} %fusion.50, bf16[2,32,256,256]{3,2,1,0:T(8,128)(2,1)} %fusion.11, f32[32,256,256]{2,1,0:T(8,128)} %param.3, bf16[256,256]{1,0:T(8,128)(2,1)S(1)} %fusion.22), kind=kOutput, calls=%fused_computation.23 | convolution fusion | flops 2176843776 | bytes 58851328 | tf_op jit(solution)/shard_map/dot_general | solution.py:30
  833.8 285.2 %all-gather.4.cloned.1.call-done = bf16[8,32,256,256]{3,2,1,0:T(8,128)(2,1)} async-done(((bf16[2,32,256,256]{3,2,1,0:T(8,128)(2,1)}), bf16[8,32,256,256]{3,2,1,0:T(8,128)(2,1)}) %all-gather.4.cloned.1.call-update) | async-done | bytes 33554448 | tf_op jit(solution)/shard_map/all_gather | solution.py:88
  1119.0 49.8 %fusion.29 = f32[2,8]{1,0:T(2,128)S(1)} fusion(bf16[8,32,256,256]{3,2,1,0:T(8,128)(2,1)} %all-gather.4.cloned.1.call-done, bf16[2,32,256,256]{3,2,1,0:T(8,128)(2,1)} %fusion.11), kind=kOutput, calls=%fused_computation.50 | convolution fusion | flops 67108864 | bytes 41943104 | tf_op jit(solution)/shard_map/dot_general | solution.py:69
  1168.8 34.6 %fusion.34 = f32[2,8]{1,0:T(2,128)S(1)} fusion(bf16[8,32,256,256]{3,2,1,0:T(8,128)(2,1)} %all-gather.4.cloned.1.call-done, bf16[2,32,256,256]{3,2,1,0:T(8,128)(2,1)S(1)} %copy-done), kind=kOutput, calls=%fused_computation.51 | convolution fusion | flops 67108864 | bytes 41943104 | tf_op jit(solution)/shard_map/dot_general | solution.py:69
  1203.4 13.8 %all-reduce = (f32[2,8]{1,0:T(2,128)S(1)}, f32[2,8]{1,0:T(2,128)S(1)}) all-reduce(f32[2,8]{1,0:T(2,128)S(1)} %fusion.29, f32[2,8]{1,0:T(2,128)S(1)} %fusion.34), channel_id=1, replica_groups=mesh['band'=4,'grid'=8] {'grid'}, use_global_device_ids=true, to_apply=%region_0.1 | all-reduce | flops 32 | bytes 256 | tf_op jit(solution)/shard_map/psum | solution.py:93
  1217.1 8.1 all-gather
  1225.3 0.6 reduce_max.9
  1225.9 0.6 broadcast_divide_fusion
  1226.7 0.1 fusion.81
  1226.8 0.1 fusion.64
  1226.9 0.1 fusion.28
  1227.1 0.1 fusion.83
  1227.2 0.1 fusion.82
  1227.3 0.1 fusion.27
  1227.5 0.1 fusion.85
  1227.6 0.1 fusion.84
  1227.8 0.1 fusion.26
  1227.9 0.1 fusion.87
  1228.0 0.1 fusion.86
  1228.2 0.1 fusion.25
  1228.3 0.1 fusion.89
  1228.4 0.1 fusion.88
  1228.6 0.1 fusion.24
  1228.7 0.2 fusion.80
  1228.9 9.1 all-gather.1
  1238.0 0.1 fusion.90
  1238.2 1.4 convolution_divide_fusion
  1239.5 31.1 %copy.105 = bf16[1,8,8192,256]{3,1,2,0:T(8,128)(2,1)} copy(bf16[1,8,8192,256]{3,2,1,0:T(8,128)(2,1)} %bitcast.162) | data formatting | bytes 67108864
  1270.6 17.5 %convolution_convert_fusion = bf16[2,2097152]{1,0:T(2,128)(2,1)} fusion(bf16[8,2097152]{1,0:T(8,128)(2,1)} %bitcast.158, bf16[8,8]{0,1:T(8,128)(2,1)S(1)} %get-tuple-element.4, s32[]{:T(128)S(6)} %select_n.21), kind=kOutput, calls=%fused_computation | convolution fusion | flops 71303168 | bytes 41943556 | tf_op jit(solution)/shard_map/dot_general | solution.py:100
  1288.1 7.9 copy.106
  (6 shorter events, 0.2 us)
Async XLA Ops:
  18.7 99.9 %all-to-all-start = ((bf16[2,32,256,256]{3,1,0,2:T(8,128)(2,1)}), bf16[2,32,256,256]{3,1,0,2:T(8,128)(2,1)}, u32[]{:S(2)}, u32[]{:S(2)}) async-start(bf16[2,32,256,256]{3,1,0,2:T(8,128)(2,1)} %copy.65), calls=%async_computation | async-start | bytes 16777216 | tf_op jit(solution)/shard_map/all_to_all | solution.py:36
  147.4 99.2 %all-to-all-start.1 = ((bf16[2,256,32,256]{3,2,0,1:T(8,128)(2,1)}), bf16[2,256,32,256]{3,2,0,1:T(8,128)(2,1)}, u32[]{:S(2)}, u32[]{:S(2)}) async-start(bf16[2,256,32,256]{3,2,0,1:T(8,128)(2,1)} %copy.68), calls=%async_computation.1 | async-start | bytes 16777216 | tf_op jit(solution)/shard_map/all_to_all | solution.py:40
  421.0 99.0 %all-to-all-start.3 = ((bf16[2,256,32,256]{3,2,0,1:T(8,128)(2,1)}), bf16[2,256,32,256]{3,2,0,1:T(8,128)(2,1)}, u32[]{:S(2)}, u32[]{:S(2)}) async-start(bf16[2,256,32,256]{3,2,0,1:T(8,128)(2,1)} %copy.75), calls=%async_computation.3 | async-start | bytes 16777216 | tf_op jit(solution)/shard_map/all_to_all | solution.py:40
  425.9 693.1 %all-gather.4.cloned.1.call-start = ((), (), s32[]{:S(2)}) async-start(), calls=%async_computation.6 | async-start | bytes 41943040 | tf_op jit(solution)/shard_map/all_gather | solution.py:88
  700.2 99.0 %all-to-all-start.5 = ((bf16[2,256,32,256]{3,2,0,1:T(8,128)(2,1)}), bf16[2,256,32,256]{3,2,0,1:T(8,128)(2,1)}, u32[]{:S(2)}, u32[]{:S(2)}) async-start(bf16[2,256,32,256]{3,2,0,1:T(8,128)(2,1)} %copy.84), calls=%async_computation.5 | async-start | bytes 16777216 | tf_op jit(solution)/shard_map/all_to_all | solution.py:40
  1119.0 49.8 %copy-start = (bf16[2,32,256,256]{3,2,1,0:T(8,128)(2,1)S(1)}, bf16[2,32,256,256]{3,2,1,0:T(8,128)(2,1)}, u32[]{:S(2)}) copy-start(bf16[2,32,256,256]{3,2,1,0:T(8,128)(2,1)} %fusion.15) | copy-start | bytes 25165828
Sparse Core Ops, SparseCore 0:
  557.5 561.5 all-gather.3
where the time goes:
time: 1310 us; the launch traced here: 1300 us
  waiting for transfers between devices  607 us (46%)
  matrix products  242 us (18%)
  blocking collectives  231 us (18%)
  local copies, waits for them, and re-layouts  186 us (14%)
  starting transfers between devices  20.7 us (2%)
  between operations  14.3 us (1%)
    all_gather x1, waiting for transfers between devices, per_device(): gathered = lax.all_gather(filtered, 'band', axis=0, tiled=True)  285 us
    all_to_all x3, waiting for transfers between devices, apply_ham(): lax.all_to_all(derived, 'grid', split_axis=1, concat_axis=2, tiled=True)  230 us
    all_to_all x2, blocking collectives, apply_ham(): lax.all_to_all(field, 'grid', split_axis=2, concat_axis=1, tiled=True)  200 us
    all_to_all x1, waiting for transfers between devices, apply_ham(): lax.all_to_all(field, 'grid', split_axis=2, concat_axis=1, tiled=True)  91.7 us
    dot_general x2, matrix products, inner_rows(): lax.dot_general(left, right, (((1,), (1,)), ((), ())), preferred_element_...  84.3 us
    dot_general x3, matrix products, apply_ham(): jnp.dot(field.reshape(-1, depth), k_z, preferred_element_type=jnp.float32)  60.8 us
    unnamed x5, local copies, waits for them, and re-layouts  50.5 us
    dot_general x3, matrix products, apply_ham(): jnp.einsum('oxjz,jy->oxyz', field, k_y, preferred_element_type=jnp.float32)  46.2 us
  transfers between devices with their start and end apart: 5, of which 5 were waited for; matrix products, arithmetic and copies ran while one was open for 10% of the time, Pallas kernels for 0%

commit v1 on v0

v1 whole, which is shorter than its diff:
```python
import functools
import math

import jax
import jax.numpy as jnp
from jax import lax
from jax.experimental import pallas as pl
from jax.experimental.pallas import tpu as pltpu
from jax.sharding import PartitionSpec as P

NS_ITERS = 6


CENTER = 9.5
HALF_WIDTH = 6.5


def second_derivative(length):
    index = jnp.arange(length, dtype=jnp.int32)
    product = index[:, None] * index[None, :] % length
    angles = product.astype(jnp.float32) * (2.0 * math.pi / length)
    freq = jnp.minimum(index, length - index).astype(jnp.float32)
    weight = -((2.0 * math.pi / length * freq) ** 2) / length
    cosines = jnp.cos(angles)
    sines = jnp.sin(angles)
    matrix = jnp.dot(cosines * weight[None, :], cosines.T, precision=lax.Precision.HIGHEST)
    matrix = matrix + jnp.dot(sines * weight[None, :], sines.T, precision=lax.Precision.HIGHEST)
    return matrix.astype(jnp.bfloat16)


def plane_kernel(mode, field_ref, term_ref, potential_ref, ky_ref, kz_ref, *rest):
    out_ref = rest[-1]
    blocks, planes, rows, depth = field_ref.shape
    for plane in range(planes):
        field = field_ref[:, plane].reshape(blocks * rows, depth)
        wide = field.astype(jnp.float32)
        term_y = jnp.dot(ky_ref[...], field, preferred_element_type=jnp.float32)
        term_z = jnp.dot(field, kz_ref[...], preferred_element_type=jnp.float32)
        term_x = term_ref[:, plane].reshape(blocks * rows, depth).astype(jnp.float32)
        result = -0.5 * (term_x + term_y + term_z) + potential_ref[plane] * wide
        if mode == 1:
            result = (result - CENTER * wide) * (1.0 / HALF_WIDTH)
        elif mode == 2:
            start = rest[0][:, plane].reshape(blocks * rows, depth).astype(jnp.float32)
            result = (result - CENTER * wide) * (2.0 / HALF_WIDTH) - start
        out_ref[:, plane] = result.astype(jnp.bfloat16).reshape(blocks, rows, depth)


def plane_call(mode, field, term, potential, k_y, k_z, start=None):
    blocks, planes, rows, depth = field.shape
    step = 2
    tall = pl.BlockSpec((blocks, step, rows, depth), lambda i: (0, i, 0, 0))
    full = lambda k: pl.BlockSpec(k.shape, lambda i: (0, 0))
    operands = [field, term, potential, k_y, k_z]
    specs = [tall, tall, pl.BlockSpec((step,) + potential.shape[1:], lambda i: (i, 0, 0)), full(k_y), full(k_z)]
    if start is not None:
        operands.append(start)
        specs.append(tall)
    size = field.size
    return pl.pallas_call(
        functools.partial(plane_kernel, mode),
        grid=(planes // step,),
        in_specs=specs,
        out_specs=tall,
        out_shape=jax.ShapeDtypeStruct(field.shape, jnp.bfloat16),
        cost_estimate=pl.CostEstimate(
            flops=2 * size * (blocks * rows + depth), bytes_accessed=size * 12, transcendentals=0
        ),
    )(*operands)


def gram_kernel(count, *refs):
    left_refs, right_refs, out_ref = refs[:count], refs[count:-1], refs[-1]

    @pl.when(pl.program_id(0) == 0)
    def _():
        out_ref[...] = jnp.zeros_like(out_ref)

    bands, planes, rows, depth = left_refs[0].shape
    for plane in range(planes):
        pick = lambda group: jnp.concatenate(
            [ref[:, plane].reshape(bands * rows, depth) for ref in group], axis=0
        )
        right = pick(right_refs)
        left = right if left_refs is right_refs else pick(left_refs)
        out_ref[...] += lax.dot_general(
            left, right, (((1,), (1,)), ((), ())), preferred_element_type=jnp.float32
        )


def gram(left, right):
    count = len(left)
    bands, planes, rows, depth = left[0].shape
    step = 4
    side = count * bands * rows
    tall = pl.BlockSpec((bands, step, rows, depth), lambda i: (0, i, 0, 0))
    size = left[0].size * count
    wide = pl.pallas_call(
        functools.partial(gram_kernel, count),
        grid=(planes // step,),
        in_specs=[tall] * (2 * count),
        out_specs=pl.BlockSpec((side, side), lambda i: (0, 0)),
        out_shape=jax.ShapeDtypeStruct((side, side), jnp.float32),
        cost_estimate=pl.CostEstimate(
            flops=2 * size * side, bytes_accessed=size * 4, transcendentals=0
        ),
    )(*left, *right)
    wide = wide.reshape(count, bands, rows, count, bands, rows)
    same = jnp.eye(rows, dtype=jnp.float32)[None, None, :, None, None, :]
    small = jnp.sum(wide * same, axis=(2, 5))
    total = count * bands
    return small.transpose(1, 0, 3, 2).reshape(total, total)


def rotate_kernel(count, mix_ref, *refs):
    bands, planes, rows, depth = refs[0].shape
    part = bands * rows
    for plane in range(planes):
        fields = jnp.concatenate(
            [ref[:, plane].reshape(part, depth) for ref in refs[:count]], axis=0
        )
        mixed = jnp.dot(mix_ref[...], fields, preferred_element_type=jnp.float32)
        for slot in range(count):
            piece = mixed[slot * part : (slot + 1) * part].astype(jnp.bfloat16)
            refs[count + slot][:, plane] = piece.reshape(bands, rows, depth)


def rotate(coeff, fields):
    count = len(fields)
    bands, planes, rows, depth = fields[0].shape
    step = 4
    side = count * bands * rows
    ordered = coeff.reshape(bands, count, bands, count).transpose(3, 2, 1, 0)
    same = jnp.eye(rows, dtype=coeff.dtype)
    mix = (ordered[:, :, None, :, :, None] * same[None, None, :, None, None, :]).reshape(side, side)
    tall = pl.BlockSpec((bands, step, rows, depth), lambda i: (0, i, 0, 0))
    size = fields[0].size * count
    return pl.pallas_call(
        functools.partial(rotate_kernel, count),
        grid=(planes // step,),
        in_specs=[pl.BlockSpec((side, side), lambda i: (0, 0))] + [tall] * count,
        out_specs=[tall] * count,
        out_shape=[jax.ShapeDtypeStruct(fields[0].shape, jnp.bfloat16)] * count,
        cost_estimate=pl.CostEstimate(
            flops=2 * size * side, bytes_accessed=size * 4, transcendentals=0
        ),
    )(mix, *fields)


def ritz(correlation, hamil):
    scale = jnp.max(jnp.sum(jnp.abs(correlation), axis=1))
    current = correlation / scale
    identity = jnp.eye(correlation.shape[0], dtype=jnp.float32)
    inverse_root = identity
    for turn_index in range(NS_ITERS):
        turn = 1.5 * identity - 0.5 * jnp.dot(
            inverse_root, current, precision=lax.Precision.HIGHEST
        )
        current = jnp.dot(current, turn, precision=lax.Precision.HIGHEST)
        inverse_root = jnp.dot(turn, inverse_root, precision=lax.Precision.HIGHEST)
    projected = (
        jnp.dot(
            jnp.dot(inverse_root.T, hamil, precision=lax.Precision.HIGHEST),
            inverse_root,
            precision=lax.Precision.HIGHEST,
        )
        / scale
    )
    return (inverse_root.astype(jnp.bfloat16), projected)


def derive_x(field, k_x):
    blocks, planes, rows, depth = field.shape
    lines = lax.all_to_all(field, "grid", split_axis=0, concat_axis=0, tiled=True)
    derived = jnp.einsum(
        "jyz,jx->xyz",
        lines.reshape(blocks * planes, rows, depth),
        k_x,
        preferred_element_type=jnp.float32,
    ).astype(jnp.bfloat16)
    return lax.all_to_all(
        derived.reshape(field.shape), "grid", split_axis=0, concat_axis=0, tiled=True
    )


def swap_bands(field):
    return lax.all_to_all(field, "band", split_axis=0, concat_axis=0, tiled=True)


def per_device(orbitals, potential):
    own, planes, height, depth = orbitals.shape
    blocks = lax.axis_size("grid")
    bands = lax.axis_size("band")
    rows = height // blocks
    k_x = second_derivative(planes * blocks)
    k_y = second_derivative(height)
    k_z = second_derivative(depth)
    starts = [
        orbitals[o].reshape(planes, blocks, rows, depth).transpose(1, 0, 2, 3) for o in range(own)
    ]
    firsts = [plane_call(1, v, derive_x(v, k_x), potential, k_y.T, k_z) for v in starts]
    filtered = [
        plane_call(2, v, derive_x(v, k_x), potential, k_y.T, k_z, start)
        for v, start in zip(firsts, starts)
    ]
    applied = [plane_call(3, v, derive_x(v, k_x), potential, k_y.T, k_z) for v in filtered]
    shape = (bands, blocks // bands * planes, rows, depth)
    mixed_f = [swap_bands(v).reshape(shape) for v in filtered]
    mixed_h = [swap_bands(v).reshape(shape) for v in applied]
    correlation = lax.psum(gram(mixed_f, mixed_f), ("band", "grid"))
    hamil = lax.psum(gram(mixed_h, mixed_f), ("band", "grid"))
    coeff, projected = ritz(correlation, hamil)
    turned = rotate(coeff, mixed_f)
    back = [
        swap_bands(v.reshape(blocks, planes, rows, depth)).transpose(1, 0, 2, 3).reshape(
            planes, height, depth
        )
        for v in turned
    ]
    return (jnp.stack(back), projected)


def solution(mesh):
    in_specs = (P("band", "grid", None, None), P("grid", None, None))
    out_specs = (P("band", "grid", None, None), P())
    return jax.shard_map(
        per_device, mesh=mesh, in_specs=in_specs, out_specs=out_specs, check_vma=False
    )
```

time: 1310 us -> 1340 us (1.023)
  matrix products: 242 us -> 39.5 us
  Pallas kernels: 0 us -> 134 us
  local copies, waits for them, and re-layouts: 186 us -> 53.8 us
  waiting for transfers between devices: 607 us -> 728 us
  blocking collectives: 231 us -> 289 us
  starting transfers between devices: 20.7 us -> 72 us
    all_to_all x4 -> x15, waiting for transfers between devices: 322 us -> 728 us  [the longest x4 322 us: swap_bands(): lax.all_to_all(field, 'band', split_axis=0, concat_axis=0, tiled=True)]
    all_gather x1 -> x0, waiting for transfers between devices: 285 us -> none  [per_device(): gathered = lax.all_gather(filtered, 'band', axis=0, tiled=True)]
    dot_general x12 -> x6, matrix products: 236 us -> 31.7 us  [derive_x(): jnp.einsum('jyz,jx->xyz', lines.reshape(blocks * planes, rows, depth), k_...]
    pallas_call x0 -> x9, Pallas kernels: none -> 134 us  [the longest x6 92.7 us: plane_call(): pl.pallas_call(functools.partial(plane_kernel, mode), grid=(planes // ste...]
    convert_element_type x8 -> x7, local copies, waits for them, and re-layouts: 93.5 us -> 27.2 us  [the longest x6 26.4 us: derive_x(): derived = jnp.einsum('jyz,jx->xyz', lines.reshape(blocks * planes, rows,...]
    all_to_all x4 -> x15, starting transfers between devices: 20.5 us -> 72 us  [the longest x6 28.3 us: derive_x(): lax.all_to_all(derived.reshape(field.shape), 'grid', split_axis=0, concat...]
    unnamed x5 -> x10, local copies, waits for them, and re-layouts: 50.5 us -> 0.02 us
    all_to_all x2 -> x3, blocking collectives: 200 us -> 250 us  [the longest x2 197 us: swap_bands(): lax.all_to_all(field, 'band', split_axis=0, concat_axis=0, tiled=True)]
  transfers between devices with their start and end apart: 5 -> 15, of which waited for: 5 -> 15; matrix products, arithmetic and copies ran while one was open for 10% -> 6% of each run, Pallas kernels for 0% -> 8%
where the time goes in v1:
time: 1340 us; the launch traced here: 1330 us
  waiting for transfers between devices  728 us (54%)
  blocking collectives  289 us (22%)
  Pallas kernels  134 us (10%)
  starting transfers between devices  72 us (5%)
  local copies, waits for them, and re-layouts  53.8 us (4%)
  matrix products  39.5 us (3%)
    all_to_all x4, waiting for transfers between devices, swap_bands(): lax.all_to_all(field, 'band', split_axis=0, concat_axis=0, tiled=True)  322 us
    all_to_all x6, waiting for transfers between devices, derive_x(): lax.all_to_all(derived.reshape(field.shape), 'grid', split_axis=0, concat...  218 us
    all_to_all x2, blocking collectives, swap_bands(): lax.all_to_all(field, 'band', split_axis=0, concat_axis=0, tiled=True)  197 us
    all_to_all x5, waiting for transfers between devices, derive_x(): lax.all_to_all(field, 'grid', split_axis=0, concat_axis=0, tiled=True)  187 us
    pallas_call x6, Pallas kernels, plane_call(): pl.pallas_call(functools.partial(plane_kernel, mode), grid=(planes // ste...  92.7 us
    all_to_all x1, blocking collectives, derive_x(): lax.all_to_all(field, 'grid', split_axis=0, concat_axis=0, tiled=True)  53.8 us
    psum x1, blocking collectives, per_device(): correlation = lax.psum(gram(mixed_f, mixed_f), ('band', 'grid'))  38.9 us
    dot_general x6, matrix products, derive_x(): jnp.einsum('jyz,jx->xyz', lines.reshape(blocks * planes, rows, depth), k_...  31.7 us
  transfers between devices with their start and end apart: 15, of which 15 were waited for; matrix products, arithmetic and copies ran while one was open for 6% of the time, Pallas kernels for 8%

profile of v1, /device:TPU:0, one launch (start us, length us, event | category | flops | bytes accessed | tf_op | source)
XLA Modules:
  0.0 1325.7 jit_solution(9139209720726944064)
XLA Ops:
  0.6 5.1 fusion.75
  5.8 2.4 copy.100
  8.2 5.2 all-to-all-start
  13.4 4.8 copy.99
  18.2 44.4 %all-to-all-done = bf16[8,32,32,256]{3,2,1,0:T(8,128)(2,1)} async-done(((bf16[8,32,32,256]{3,2,1,0:T(8,128)(2,1)}), bf16[8,32,32,256]{3,2,1,0:T(8,128)(2,1)}, u32[]{:S(2)}, u32[]{:S(2)}) %all-to-all-start) | async-done | bytes 4194336 | tf_op jit(solution)/shard_map/all_to_all | solution.py:174
  62.6 4.6 all-to-all-start.5
  68.5 1.4 fusion.30.kz_ref
  69.9 5.3 fusion.12
  75.2 4.4 copy.50
  79.7 36.6 %all-to-all-done.5 = bf16[8,32,32,256]{3,2,1,0:T(8,128)(2,1)} async-done(((bf16[8,32,32,256]{3,2,1,0:T(8,128)(2,1)}), bf16[8,32,32,256]{3,2,1,0:T(8,128)(2,1)}, u32[]{:S(2)}, u32[]{:S(2)}) %all-to-all-start.5) | async-done | bytes 4194336 | tf_op jit(solution)/shard_map/all_to_all | solution.py:174
  116.3 4.9 all-to-all-start.1
  121.2 5.3 fusion.18
  126.5 4.4 copy.57
  130.8 39.5 %all-to-all-done.1.term_ref = bf16[8,32,32,256]{3,2,1,0:T(8,128)(2,1)} async-done(((bf16[8,32,32,256]{3,2,1,0:T(8,128)(2,1)}), bf16[8,32,32,256]{3,2,1,0:T(8,128)(2,1)}, u32[]{:S(2)}, u32[]{:S(2)}) %all-to-all-start.1) | async-done | bytes 4194336 | tf_op jit(solution)/shard_map/all_to_all | solution.py:181
  170.3 4.6 all-to-all-start.6
  175.7 15.2 %shard_map.41.field_ref = bf16[8,32,32,256]{3,2,1,0:T(8,128)(2,1)} custom-call(bf16[8,32,32,256]{3,2,1,0:T(8,128)(2,1)} %bitcast.89, bf16[8,32,32,256]{3,2,1,0:T(8,128)(2,1)} %all-to-all-done.1.term_ref, f32[32,256,256]{2,1,0:T(8,128)} %potential_ref.11, bf16[256,256]{1,0:T(8,128)(2,1)} %copy.51.ky_ref, bf16[256,256]{1,0:T(8,128)(2,1)} %copy-done.1), custom_call_target="tpu_custom_call" | custom-call | flops 2147483648 | bytes 25165824 | tf_op jit(solution)/shard_map/pallas_call | solution.py:60
  190.9 33.1 %all-to-all-done.6.term_ref = bf16[8,32,32,256]{3,2,1,0:T(8,128)(2,1)} async-done(((bf16[8,32,32,256]{3,2,1,0:T(8,128)(2,1)}), bf16[8,32,32,256]{3,2,1,0:T(8,128)(2,1)}, u32[]{:S(2)}, u32[]{:S(2)}) %all-to-all-start.6) | async-done | bytes 4194336 | tf_op jit(solution)/shard_map/all_to_all | solution.py:181
  224.0 4.6 all-to-all-start.2
  228.6 15.2 %shard_map.43.field_ref = bf16[8,32,32,256]{3,2,1,0:T(8,128)(2,1)} custom-call(bf16[8,32,32,256]{3,2,1,0:T(8,128)(2,1)} %bitcast.86, bf16[8,32,32,256]{3,2,1,0:T(8,128)(2,1)} %all-to-all-done.6.term_ref, f32[32,256,256]{2,1,0:T(8,128)} %potential_ref.11, bf16[256,256]{1,0:T(8,128)(2,1)} %copy.51.ky_ref, bf16[256,256]{1,0:T(8,128)(2,1)} %copy-done.1), custom_call_target="tpu_custom_call" | custom-call | flops 2147483648 | bytes 25165824 | tf_op jit(solution)/shard_map/pallas_call | solution.py:60
  243.9 33.8 %all-to-all-done.2 = bf16[8,32,32,256]{3,2,1,0:T(8,128)(2,1)} async-done(((bf16[8,32,32,256]{3,2,1,0:T(8,128)(2,1)}), bf16[8,32,32,256]{3,2,1,0:T(8,128)(2,1)}, u32[]{:S(2)}, u32[]{:S(2)}) %all-to-all-start.2) | async-done | bytes 4194336 | tf_op jit(solution)/shard_map/all_to_all | solution.py:174
  277.7 4.6 all-to-all-start.7
  282.3 5.3 fusion.15
  287.6 4.4 copy.53
  291.9 39.4 %all-to-all-done.7 = bf16[8,32,32,256]{3,2,1,0:T(8,128)(2,1)} async-done(((bf16[8,32,32,256]{3,2,1,0:T(8,128)(2,1)}), bf16[8,32,32,256]{3,2,1,0:T(8,128)(2,1)}, u32[]{:S(2)}, u32[]{:S(2)}) %all-to-all-start.7) | async-done | bytes 4194336 | tf_op jit(solution)/shard_map/all_to_all | solution.py:174
  331.4 5.1 all-to-all-start.3
  336.5 5.3 fusion.21
  341.8 4.4 copy.60
  346.2 39.4 %all-to-all-done.3.term_ref = bf16[8,32,32,256]{3,2,1,0:T(8,128)(2,1)} async-done(((bf16[8,32,32,256]{3,2,1,0:T(8,128)(2,1)}), bf16[8,32,32,256]{3,2,1,0:T(8,128)(2,1)}, u32[]{:S(2)}, u32[]{:S(2)}) %all-to-all-start.3) | async-done | bytes 4194336 | tf_op jit(solution)/shard_map/all_to_all | solution.py:181
  385.6 4.6 all-to-all-start.8
  390.2 16.3 %shard_map.42.field_ref = bf16[8,32,32,256]{3,2,1,0:T(8,128)(2,1)} custom-call(bf16[8,32,32,256]{3,2,1,0:T(8,128)(2,1)} %shard_map.41.field_ref, bf16[8,32,32,256]{3,2,1,0:T(8,128)(2,1)} %all-to-all-done.3.term_ref, f32[32,256,256]{2,1,0:T(8,128)} %potential_ref.11, bf16[256,256]{1,0:T(8,128)(2,1)} %copy.51.ky_ref, bf16[256,256]{1,0:T(8,128)(2,1)} %copy-done.1, ...), custom_call_target="tpu_custom_call" | custom-call | flops 2147483648 | bytes 25165824 | tf_op jit(solution)/shard_map/pallas_call | solution.py:60
  406.4 32.8 %all-to-all-done.8.term_ref = bf16[8,32,32,256]{3,2,1,0:T(8,128)(2,1)} async-done(((bf16[8,32,32,256]{3,2,1,0:T(8,128)(2,1)}), bf16[8,32,32,256]{3,2,1,0:T(8,128)(2,1)}, u32[]{:S(2)}, u32[]{:S(2)}) %all-to-all-start.8) | async-done | bytes 4194336 | tf_op jit(solution)/shard_map/all_to_all | solution.py:181
  439.3 4.6 all-to-all-start.12
  443.9 16.2 %shard_map.44.field_ref = bf16[8,32,32,256]{3,2,1,0:T(8,128)(2,1)} custom-call(bf16[8,32,32,256]{3,2,1,0:T(8,128)(2,1)} %shard_map.43.field_ref, bf16[8,32,32,256]{3,2,1,0:T(8,128)(2,1)} %all-to-all-done.8.term_ref, f32[32,256,256]{2,1,0:T(8,128)} %potential_ref.11, bf16[256,256]{1,0:T(8,128)(2,1)} %copy.51.ky_ref, bf16[256,256]{1,0:T(8,128)(2,1)} %copy-done.1, ...), custom_call_target="tpu_custom_call" | custom-call | flops 2147483648 | bytes 25165824 | tf_op jit(solution)/shard_map/pallas_call | solution.py:60
  460.1 32.9 %all-to-all-done.12 = bf16[8,32,32,256]{3,2,1,0:T(8,128)(2,1)} async-done(((bf16[8,32,32,256]{3,2,1,0:T(8,128)(2,1)}), bf16[8,32,32,256]{3,2,1,0:T(8,128)(2,1)}, u32[]{:S(2)}, u32[]{:S(2)}) %all-to-all-start.12) | async-done | bytes 4194336 | tf_op jit(solution)/shard_map/all_to_all | solution.py:174
  493.0 53.8 %all_to_all.90 = bf16[8,32,32,256]{3,2,1,0:T(8,128)(2,1)} all-to-all(bf16[8,32,32,256]{3,2,1,0:T(8,128)(2,1)} %shard_map.44.field_ref), channel_id=1, replica_groups=mesh['band'=4,'grid'=8] {'grid'}, dimensions={0} | all-to-all | bytes 8388608 | tf_op jit(solution)/shard_map/all_to_all | solution.py:174
  546.8 98.2 %all_to_all.91 = bf16[8,32,32,256]{3,2,1,0:T(8,128)(2,1)} all-to-all(bf16[8,32,32,256]{3,2,1,0:T(8,128)(2,1)S(1)} %copy-done), channel_id=1, replica_groups=mesh['band'=4,'grid'=8] {'band'}, dimensions={0} | all-to-all | bytes 8388608 | tf_op jit(solution)/shard_map/all_to_all | solution.py:187
  644.9 5.2 all-to-all-start.9
  650.1 5.3 fusion.24
  655.4 4.4 copy.67
  659.8 82.5 %all-to-all-done.9 = bf16[8,32,32,256]{3,2,1,0:T(8,128)(2,1)} async-done(((bf16[8,32,32,256]{3,2,1,0:T(8,128)(2,1)}), bf16[8,32,32,256]{3,2,1,0:T(8,128)(2,1)}, u32[]{:S(2)}, u32[]{:S(2)}) %all-to-all-start.9) | async-done | bytes 4194336 | tf_op jit(solution)/shard_map/all_to_all | solution.py:187
  742.3 4.6 all-to-all-start.13
  746.9 5.3 fusion.27
  752.2 4.4 copy.70
  756.6 39.4 %all-to-all-done.13.term_ref = bf16[8,32,32,256]{3,2,1,0:T(8,128)(2,1)} async-done(((bf16[8,32,32,256]{3,2,1,0:T(8,128)(2,1)}), bf16[8,32,32,256]{3,2,1,0:T(8,128)(2,1)}, u32[]{:S(2)}, u32[]{:S(2)}) %all-to-all-start.13) | async-done | bytes 4194336 | tf_op jit(solution)/shard_map/all_to_all | solution.py:181
  796.0 4.6 all-to-all-start.16
  800.5 14.9 %shard_map.47 = bf16[8,32,32,256]{3,2,1,0:T(8,128)(2,1)} custom-call(bf16[8,32,32,256]{3,2,1,0:T(8,128)(2,1)} %shard_map.42.field_ref, bf16[8,32,32,256]{3,2,1,0:T(8,128)(2,1)} %all-to-all-done.13.term_ref, f32[32,256,256]{2,1,0:T(8,128)} %potential_ref.11, bf16[256,256]{1,0:T(8,128)(2,1)} %copy.51.ky_ref, bf16[256,256]{1,0:T(8,128)(2,1)} %copy-done.1), custom_call_target="tpu_custom_call" | custom-call | flops 2147483648 | bytes 25165824 | tf_op jit(solution)/shard_map/pallas_call | solution.py:60
  815.4 34.2 %all-to-all-done.16.term_ref = bf16[8,32,32,256]{3,2,1,0:T(8,128)(2,1)} async-done(((bf16[8,32,32,256]{3,2,1,0:T(8,128)(2,1)}), bf16[8,32,32,256]{3,2,1,0:T(8,128)(2,1)}, u32[]{:S(2)}, u32[]{:S(2)}) %all-to-all-start.16) | async-done | bytes 4194336 | tf_op jit(solution)/shard_map/all_to_all | solution.py:181
  849.6 4.9 all-to-all-start.14
  854.6 14.9 %shard_map.48 = bf16[8,32,32,256]{3,2,1,0:T(8,128)(2,1)} custom-call(bf16[8,32,32,256]{3,2,1,0:T(8,128)(2,1)} %shard_map.44.field_ref, bf16[8,32,32,256]{3,2,1,0:T(8,128)(2,1)} %all-to-all-done.16.term_ref, f32[32,256,256]{2,1,0:T(8,128)} %potential_ref.11, bf16[256,256]{1,0:T(8,128)(2,1)} %copy.51.ky_ref, bf16[256,256]{1,0:T(8,128)(2,1)} %copy-done.1), custom_call_target="tpu_custom_call" | custom-call | flops 2147483648 | bytes 25165824 | tf_op jit(solution)/shard_map/pallas_call | solution.py:60
  869.4 75.7 %all-to-all-done.14 = bf16[8,32,32,256]{3,2,1,0:T(8,128)(2,1)} async-done(((bf16[8,32,32,256]{3,2,1,0:T(8,128)(2,1)}), bf16[8,32,32,256]{3,2,1,0:T(8,128)(2,1)}, u32[]{:S(2)}, u32[]{:S(2)}) %all-to-all-start.14) | async-done | bytes 4194336 | tf_op jit(solution)/shard_map/all_to_all | solution.py:187
  945.1 5.2 all-to-all-start.17
  950.3 13.9 %shard_map.45 = f32[256,256]{1,0:T(8,128)} custom-call(bf16[4,64,32,256]{3,2,1,0:T(8,128)(2,1)} %bitcast.81, bf16[4,64,32,256]{3,2,1,0:T(8,128)(2,1)} %bitcast.15.refs_1_.refs_3_, bf16[4,64,32,256]{3,2,1,0:T(8,128)(2,1)} %bitcast.82, bf16[4,64,32,256]{3,2,1,0:T(8,128)(2,1)} %bitcast.15.refs_1_.refs_3_), custom_call_target="tpu_custom_call" | custom-call | flops 2147483648 | bytes 16777216 | tf_op jit(solution)/shard_map/pallas_call | solution.py:98
  964.2 1.4 reshape.112
  965.6 77.4 %all-to-all-done.17 = bf16[8,32,32,256]{3,2,1,0:T(8,128)(2,1)} async-done(((bf16[8,32,32,256]{3,2,1,0:T(8,128)(2,1)}), bf16[8,32,32,256]{3,2,1,0:T(8,128)(2,1)}, u32[]{:S(2)}, u32[]{:S(2)}) %all-to-all-start.17) | async-done | bytes 4194336 | tf_op jit(solution)/shard_map/all_to_all | solution.py:187
  1043.0 13.9 %shard_map.49 = f32[256,256]{1,0:T(8,128)} custom-call(bf16[4,64,32,256]{3,2,1,0:T(8,128)(2,1)} %bitcast.26.refs_0_, bf16[4,64,32,256]{3,2,1,0:T(8,128)(2,1)} %bitcast.29.refs_1_, bf16[4,64,32,256]{3,2,1,0:T(8,128)(2,1)} %bitcast.83, bf16[4,64,32,256]{3,2,1,0:T(8,128)(2,1)} %bitcast.15.refs_1_.refs_3_), custom_call_target="tpu_custom_call" | custom-call | flops 2147483648 | bytes 16777216 | tf_op jit(solution)/shard_map/pallas_call | solution.py:98
  1056.9 1.4 reshape.123
  1059.4 38.9 %all-reduce = (f32[8,8]{1,0:T(8,128)S(1)}, f32[8,8]{1,0:T(8,128)S(1)}) all-reduce(f32[8,8]{1,0:T(8,128)S(1)} %reshape.113, f32[8,8]{1,0:T(8,128)S(1)} %reshape.124), channel_id=1, replica_groups=mesh['band'=4,'grid'=8] {'band','grid'}, use_global_device_ids=true, to_apply=%region_1.2 | all-reduce | flops 128 | bytes 1024 | tf_op jit(solution)/shard_map/psum | solution.py:210
  1104.2 13.8 %shard_map.46 = (bf16[4,64,32,256]{3,2,1,0:T(8,128)(2,1)}, bf16[4,64,32,256]{3,2,1,0:T(8,128)(2,1)}) custom-call(bf16[256,256]{1,0:T(8,128)(2,1)} %mul.188.mix_ref, bf16[4,64,32,256]{3,2,1,0:T(8,128)(2,1)} %bitcast.84, bf16[4,64,32,256]{3,2,1,0:T(8,128)(2,1)} %bitcast.15.refs_1_.refs_3_), custom_call_target="tpu_custom_call" | custom-call | flops 2147483648 | bytes 16777216 | tf_op jit(solution)/shard_map/pallas_call | solution.py:138
  1117.9 98.5 %all_to_all.92 = bf16[8,32,32,256]{3,2,1,0:T(8,128)(2,1)} all-to-all(bf16[8,32,32,256]{3,2,1,0:T(8,128)(2,1)} %bitcast.105), channel_id=1, replica_groups=mesh['band'=4,'grid'=8] {'band'}, dimensions={0} | all-to-all | bytes 8388608 | tf_op jit(solution)/shard_map/all_to_all | solution.py:187
  1216.5 4.9 all-to-all-start.10
  1222.9 4.8 copy.65
  1227.7 86.4 %all-to-all-done.10 = bf16[8,32,32,256]{3,2,1,0:T(8,128)(2,1)} async-done(((bf16[8,32,32,256]{3,2,1,0:T(8,128)(2,1)}), bf16[8,32,32,256]{3,2,1,0:T(8,128)(2,1)}, u32[]{:S(2)}, u32[]{:S(2)}) %all-to-all-start.10) | async-done | bytes 4194336 | tf_op jit(solution)/shard_map/all_to_all | solution.py:187
  1314.1 5.0 copy.64
  1319.1 6.3 pad_maximum_fusion
  (45 shorter events, 10.6 us)
Async XLA Ops:
  8.2 54.4 %all-to-all-start = ((bf16[8,32,32,256]{3,2,1,0:T(8,128)(2,1)}), bf16[8,32,32,256]{3,2,1,0:T(8,128)(2,1)}, u32[]{:S(2)}, u32[]{:S(2)}) async-start(bf16[8,32,32,256]{3,2,1,0:T(8,128)(2,1)} %bitcast.88), calls=%async_computation | async-start | bytes 8388608 | tf_op jit(solution)/shard_map/all_to_all | solution.py:174
  62.6 53.7 %all-to-all-start.5 = ((bf16[8,32,32,256]{3,2,1,0:T(8,128)(2,1)}), bf16[8,32,32,256]{3,2,1,0:T(8,128)(2,1)}, u32[]{:S(2)}, u32[]{:S(2)}) async-start(bf16[8,32,32,256]{3,2,1,0:T(8,128)(2,1)} %bitcast.85), calls=%async_computation.5 | async-start | bytes 8388608 | tf_op jit(solution)/shard_map/all_to_all | solution.py:174
  69.9 105.0 %copy-start.1 = (bf16[256,256]{1,0:T(8,128)(2,1)}, bf16[256,256]{1,0:T(8,128)(2,1)S(1)}, u32[]{:S(2)}) copy-start(bf16[256,256]{1,0:T(8,128)(2,1)S(1)} %fusion.30.kz_ref) | copy-start | bytes 393220
  116.3 54.0 %all-to-all-start.1 = ((bf16[8,32,32,256]{3,2,1,0:T(8,128)(2,1)}), bf16[8,32,32,256]{3,2,1,0:T(8,128)(2,1)}, u32[]{:S(2)}, u32[]{:S(2)}) async-start(bf16[8,32,32,256]{3,2,1,0:T(8,128)(2,1)} %bitcast.95), calls=%async_computation.1 | async-start | bytes 8388608 | tf_op jit(solution)/shard_map/all_to_all | solution.py:181
  170.3 53.7 %all-to-all-start.6 = ((bf16[8,32,32,256]{3,2,1,0:T(8,128)(2,1)}), bf16[8,32,32,256]{3,2,1,0:T(8,128)(2,1)}, u32[]{:S(2)}, u32[]{:S(2)}) async-start(bf16[8,32,32,256]{3,2,1,0:T(8,128)(2,1)} %bitcast.96), calls=%async_computation.6 | async-start | bytes 8388608 | tf_op jit(solution)/shard_map/all_to_all | solution.py:181
  224.0 53.7 %all-to-all-start.2 = ((bf16[8,32,32,256]{3,2,1,0:T(8,128)(2,1)}), bf16[8,32,32,256]{3,2,1,0:T(8,128)(2,1)}, u32[]{:S(2)}, u32[]{:S(2)}) async-start(bf16[8,32,32,256]{3,2,1,0:T(8,128)(2,1)} %shard_map.41.field_ref), calls=%async_computation.2 | async-start | bytes 8388608 | tf_op jit(solution)/shard_map/all_to_all | solution.py:174
  243.9 38.4 %copy-start.2 = (bf16[256,256]{1,0:T(8,128)(2,1)S(1)}, bf16[256,256]{1,0:T(8,128)(2,1)}, u32[]{:S(2)}) copy-start(bf16[256,256]{1,0:T(8,128)(2,1)} %copy-done.1) | copy-start | bytes 393220
  277.7 53.7 %all-to-all-start.7 = ((bf16[8,32,32,256]{3,2,1,0:T(8,128)(2,1)}), bf16[8,32,32,256]{3,2,1,0:T(8,128)(2,1)}, u32[]{:S(2)}, u32[]{:S(2)}) async-start(bf16[8,32,32,256]{3,2,1,0:T(8,128)(2,1)} %shard_map.43.field_ref), calls=%async_computation.7 | async-start | bytes 8388608 | tf_op jit(solution)/shard_map/all_to_all | solution.py:174
  331.4 54.2 %all-to-all-start.3 = ((bf16[8,32,32,256]{3,2,1,0:T(8,128)(2,1)}), bf16[8,32,32,256]{3,2,1,0:T(8,128)(2,1)}, u32[]{:S(2)}, u32[]{:S(2)}) async-start(bf16[8,32,32,256]{3,2,1,0:T(8,128)(2,1)} %bitcast.97), calls=%async_computation.3 | async-start | bytes 8388608 | tf_op jit(solution)/shard_map/all_to_all | solution.py:181
  385.6 53.7 %all-to-all-start.8 = ((bf16[8,32,32,256]{3,2,1,0:T(8,128)(2,1)}), bf16[8,32,32,256]{3,2,1,0:T(8,128)(2,1)}, u32[]{:S(2)}, u32[]{:S(2)}) async-start(bf16[8,32,32,256]{3,2,1,0:T(8,128)(2,1)} %bitcast.94), calls=%async_computation.8 | async-start | bytes 8388608 | tf_op jit(solution)/shard_map/all_to_all | solution.py:181
  439.3 53.7 %all-to-all-start.12 = ((bf16[8,32,32,256]{3,2,1,0:T(8,128)(2,1)}), bf16[8,32,32,256]{3,2,1,0:T(8,128)(2,1)}, u32[]{:S(2)}, u32[]{:S(2)}) async-start(bf16[8,32,32,256]{3,2,1,0:T(8,128)(2,1)} %shard_map.42.field_ref), calls=%async_computation.12 | async-start | bytes 8388608 | tf_op jit(solution)/shard_map/all_to_all | solution.py:174
  493.0 53.8 %copy-start = (bf16[8,32,32,256]{3,2,1,0:T(8,128)(2,1)S(1)}, bf16[8,32,32,256]{3,2,1,0:T(8,128)(2,1)}, u32[]{:S(2)}) copy-start(bf16[8,32,32,256]{3,2,1,0:T(8,128)(2,1)} %shard_map.42.field_ref) | copy-start | bytes 12582916
  644.9 5.2 copy-start.3
  644.9 97.4 %all-to-all-start.9 = ((bf16[8,32,32,256]{3,2,1,0:T(8,128)(2,1)}), bf16[8,32,32,256]{3,2,1,0:T(8,128)(2,1)}, u32[]{:S(2)}, u32[]{:S(2)}) async-start(bf16[8,32,32,256]{3,2,1,0:T(8,128)(2,1)} %shard_map.44.field_ref), calls=%async_computation.9 | async-start | bytes 8388608 | tf_op jit(solution)/shard_map/all_to_all | solution.py:187
  742.3 53.7 %all-to-all-start.13 = ((bf16[8,32,32,256]{3,2,1,0:T(8,128)(2,1)}), bf16[8,32,32,256]{3,2,1,0:T(8,128)(2,1)}, u32[]{:S(2)}, u32[]{:S(2)}) async-start(bf16[8,32,32,256]{3,2,1,0:T(8,128)(2,1)} %bitcast.98), calls=%async_computation.13 | async-start | bytes 8388608 | tf_op jit(solution)/shard_map/all_to_all | solution.py:181
  796.0 53.7 %all-to-all-start.16 = ((bf16[8,32,32,256]{3,2,1,0:T(8,128)(2,1)}), bf16[8,32,32,256]{3,2,1,0:T(8,128)(2,1)}, u32[]{:S(2)}, u32[]{:S(2)}) async-start(bf16[8,32,32,256]{3,2,1,0:T(8,128)(2,1)} %bitcast.99), calls=%async_computation.16 | async-start | bytes 8388608 | tf_op jit(solution)/shard_map/all_to_all | solution.py:181
  849.6 95.5 %all-to-all-start.14 = ((bf16[8,32,32,256]{3,2,1,0:T(8,128)(2,1)}), bf16[8,32,32,256]{3,2,1,0:T(8,128)(2,1)}, u32[]{:S(2)}, u32[]{:S(2)}) async-start(bf16[8,32,32,256]{3,2,1,0:T(8,128)(2,1)} %shard_map.47), calls=%async_computation.14 | async-start | bytes 8388608 | tf_op jit(solution)/shard_map/all_to_all | solution.py:187
  945.1 97.9 %all-to-all-start.17 = ((bf16[8,32,32,256]{3,2,1,0:T(8,128)(2,1)}), bf16[8,32,32,256]{3,2,1,0:T(8,128)(2,1)}, u32[]{:S(2)}, u32[]{:S(2)}) async-start(bf16[8,32,32,256]{3,2,1,0:T(8,128)(2,1)} %shard_map.48), calls=%async_computation.17 | async-start | bytes 8388608 | tf_op jit(solution)/shard_map/all_to_all | solution.py:187
  1216.5 97.6 %all-to-all-start.10 = ((bf16[8,32,32,256]{3,2,1,0:T(8,128)(2,1)}), bf16[8,32,32,256]{3,2,1,0:T(8,128)(2,1)}, u32[]{:S(2)}, u32[]{:S(2)}) async-start(bf16[8,32,32,256]{3,2,1,0:T(8,128)(2,1)} %bitcast.104), calls=%async_computation.10 | async-start | bytes 8388608 | tf_op jit(solution)/shard_map/all_to_all | solution.py:187
  1314.1 5.0 copy-start.4
